TPU v7x, 32 devices: a whole 2x2x4 slice. The times are simulated.
32 devices in a mesh: pole: 4 (over y, x), node: 8 (over z, core).
Axes of the slice: x: 2, y: 2, z: 4, core: 2. Of those that a mesh axis runs over, the one named last changes fastest.
Arguments:
- dens_part: bfloat16 [4, 32768, 338], P('pole', 'node'), may hold values from -1.5 to 1.5
- dest_node: int32 [32768], P('node'), may hold values from 0 to 7, as said below
- pair_slot: int32 [32768], P('node'), may hold values from 0 to 1023, as said below
- deriv: bfloat16 [32768, 1014], P(('pole', 'node')), may hold values from -0.119628906 to 0.119628906
- pair_atoms: int32 [2, 32768], P(None, ('pole', 'node')), may hold values from 0 to 4095
Outputs:
- forces: float32 [3, 4096], P(None, ('pole', 'node'))
Inputs may be any that keep to these rules, and one draw needn't show every extreme that they name: The share of block s is (s // 1024) % 4. Of the 1024 blocks of one share at most 256 have the same dest_node, and in every share exactly 256 do for some node index. Within one pole index, the number of blocks that a share on node n sends to node (n + k) % 8 depends on k alone. Every pair of pole index p and node index m receives exactly 1024 blocks of share p. `pair_slot`: the blocks of share p with dest_node m take each position of 0 to 1023 exactly once.
All inputs are finite; a program needn't handle non-finite values.
Results may differ from a plain program's by a relative error of at most 0.009.
Values may be sent and summed in bfloat16 or wider, within the bound.
A program may use at most 64 MiB of HBM per device.

v0:
```python
import jax
import jax.numpy as jnp
from jax import lax
from jax.sharding import PartitionSpec as P

ATOM_DEV = 128


def body(dens_part, dest_node, pair_slot, deriv, pair_atoms):
    blocks_here = deriv.shape[0]
    width = dens_part.shape[2]
    half_width = width // 2
    nodes = lax.axis_size("node")
    poles = lax.axis_size("pole")
    pole_here = lax.axis_index("pole")
    capacity = 2 * blocks_here // nodes
    partials = dens_part[0]
    share_sum = lax.psum_scatter(partials, "pole", scatter_dimension=0, tiled=True).astype(
        jnp.float32
    )
    density = share_sum.astype(jnp.bfloat16)
    target_node = lax.dynamic_slice_in_dim(dest_node, pole_here * blocks_here, blocks_here, 0)
    target_slot = lax.dynamic_slice_in_dim(pair_slot, pole_here * blocks_here, blocks_here, 0)
    onehot = (target_node[:, None] == jnp.arange(nodes, dtype=jnp.int32)[None, :]).astype(jnp.int32)
    slot_rank = jnp.sum((jnp.cumsum(onehot, axis=0) - onehot) * onehot, axis=1)
    placement_row = target_node * capacity + slot_rank
    outgoing = jnp.zeros((nodes * capacity, width), jnp.bfloat16).at[placement_row].set(density)
    sent_slot = (
        jnp.full((nodes * capacity,), blocks_here, jnp.int32).at[placement_row].set(target_slot)
    )
    arrived, recv_slot = (
        lax.all_to_all(
            outgoing.reshape(nodes, capacity, width),
            "node",
            split_axis=0,
            concat_axis=0,
            tiled=True,
        ),
        lax.all_to_all(
            sent_slot.reshape(nodes, capacity), "node", split_axis=0, concat_axis=0, tiled=True
        ),
    )
    pair_dens = (
        jnp.zeros((blocks_here, width), jnp.bfloat16)
        .at[recv_slot.reshape(-1)]
        .set(arrived.reshape(-1, width), mode="drop")
    )
    grad_h = deriv[:, : 3 * half_width].reshape(blocks_here, 3, half_width)
    grad_s = deriv[:, 3 * half_width :].reshape(blocks_here, 3, half_width)
    first = jnp.einsum(
        "bk,bck->bc", pair_dens[:, :half_width], grad_h, preferred_element_type=jnp.float32
    )
    second = jnp.einsum(
        "bk,bck->bc", pair_dens[:, half_width:], grad_s, preferred_element_type=jnp.float32
    )
    pair_term = first - second
    atoms_total = ATOM_DEV * poles * nodes
    partial_forces = jnp.zeros((3, atoms_total), jnp.float32)
    partial_forces = partial_forces.at[:, pair_atoms[0]].add(-2.0 * pair_term.T)
    partial_forces = partial_forces.at[:, pair_atoms[1]].add(2.0 * pair_term.T)
    return lax.psum_scatter(partial_forces, ("pole", "node"), scatter_dimension=1, tiled=True)


def solution(mesh):
    return jax.shard_map(
        body,
        mesh=mesh,
        in_specs=(
            P("pole", "node", None),
            P("node"),
            P("node"),
            P(("pole", "node"), None),
            P(None, ("pole", "node")),
        ),
        out_specs=P(None, ("pole", "node")),
        check_vma=False,
    )
```

profile of v0, /device:TPU:0, one launch (start us, length us, event | category | flops | bytes accessed | tf_op | source)
XLA Modules:
  0.0 276.1 jit_solution(1843825718476574322)
XLA Ops:
  6.5 0.7 reduce-scatter.3.cloned.1.call-update
  7.3 2.3 reduce-window.6
  9.6 0.3 slice_reduce_fusion
  9.9 0.2 reduce-window.9
  10.0 0.7 dynamic_slice.7
  10.7 0.1 add_bitcast_fusion
  10.9 4.9 %scatter_custom_fusion = s32[2048]{0:T(1024)} fusion(s32[1024]{0:T(1024)S(1)} %compare_select_fusion.3, s32[1024]{0:T(1024)S(1)} %dynamic_slice.7, s32[]{:T(128)} %constant.14.clone.1), kind=kCustom, calls=%fused_computation.37 | custom fusion | bytes 8196 | tf_op jit(solution)/shard_map/scatter | solution.py:29
  15.7 6.4 %all-to-all-start = ((s32[8,1,256]{2,1,0:T(1,128)}), s32[8,1,256]{2,1,0:T(1,128)S(1)}, u32[]{:S(2)}, u32[]{:S(2)}) async-start(s32[8,1,256]{2,1,0:T(1,128)} %bitcast.4), calls=%async_computation | async-start | bytes 16384 | tf_op jit(solution)/shard_map/all_to_all | solution.py:39
  22.1 32.2 %reduce-scatter.3.cloned.1.call-done = bf16[1024,338]{0,1:T(8,128)(2,1)} async-done(((bf16[4096,338]{0,1:T(8,128)(2,1)}), bf16[1024,338]{0,1:T(8,128)(2,1)}) %reduce-scatter.3.cloned.1.call-update) | async-done | bytes 692240 | tf_op jit(solution)/shard_map/reduce_scatter | solution.py:18
  54.3 1.5 copy.16
  55.8 5.5 %scatter_custom_fusion.1 = bf16[2048,338]{1,0:T(8,128)(2,1)S(1)} fusion(s32[1024]{0:T(1024)S(1)} %compare_select_fusion.3, bf16[1024,338]{1,0:T(8,128)(2,1)S(1)} %copy.16, bf16[]{:T(256)} %constant.13.clone.1), kind=kCustom, calls=%fused_computation.11 | custom fusion | bytes 1384450 | tf_op jit(solution)/shard_map/scatter | solution.py:27
  61.3 1.6 copy.17
  62.9 4.6 %all-to-all-start.1 = ((bf16[8,256,338]{1,2,0:T(8,128)(2,1)}), bf16[8,256,338]{1,2,0:T(8,128)(2,1)S(1)}, u32[]{:S(2)}, u32[]{:S(2)}) async-start(bf16[8,256,338]{1,2,0:T(8,128)(2,1)} %copy.17), calls=%async_computation.2 | async-start | bytes 2818048 | tf_op jit(solution)/shard_map/all_to_all | solution.py:32
  67.5 0.0 reduce-scatter.5.cloned.1.call-start
  67.6 2.9 %fusion.23 = (bf16[1024,507]{0,1:T(8,128)(2,1)}, bf16[1024,507]{0,1:T(8,128)(2,1)S(1)}) fusion(bf16[1024,1014]{0,1:T(8,128)(2,1)} %param.8), kind=kLoop, calls=%fused_computation.39 | loop fusion | bytes 4153344 | tf_op jit(solution)/shard_map/slice | solution.py:49
  70.5 1.5 reshape.125
  72.0 2.5 copy.25
  74.5 0.3 reshape.124
  74.8 2.5 copy.22
  77.4 24.4 %all-to-all-done.1 = bf16[8,256,338]{1,2,0:T(8,128)(2,1)S(1)} async-done(((bf16[8,256,338]{1,2,0:T(8,128)(2,1)}), bf16[8,256,338]{1,2,0:T(8,128)(2,1)S(1)}, u32[]{:S(2)}, u32[]{:S(2)}) %all-to-all-start.1) | async-done | bytes 1384480 | tf_op jit(solution)/shard_map/all_to_all | solution.py:32
  101.8 1.6 copy.27
  103.4 10.3 %scatter_custom_fusion.2 = bf16[1024,338]{1,0:T(8,128)(2,1)S(1)} fusion(s32[2048]{0:T(1024)S(1)} %bitcast.56, bf16[2048,338]{1,0:T(8,128)(2,1)} %bitcast.53, bf16[]{:T(256)} %constant.13.clone.1), kind=kCustom, calls=%fused_computation.18 | custom fusion | bytes 692736 | tf_op jit(solution)/shard_map/scatter | solution.py:46
  113.6 0.3 slice_bitcast_fusion
  113.9 1.2 fusion.2
  115.1 0.4 copy-done.2
  115.5 1.2 fusion.4
  116.7 6.6 %scatter_custom_fusion.3 = f32[3,4096]{0,1:T(8,128)S(1)} fusion(s32[1024]{0:T(1024)S(1)} %bitcast.58, f32[]{:T(128)} %constant.10.clone.1, f32[]{:T(128)} %constant.6.clone.1, f32[1024,3]{1,0:T(8,128)S(1)} %bitcast.51, f32[1024,3]{1,0:T(8,128)S(1)} %bitcast.49), kind=kCustom, calls=%fused_computation.5 | custom fusion | flops 9216 | bytes 1097736 | tf_op jit(solution)/shard_map/scatter-add | solution.py:59
  123.3 6.3 %scatter_custom_fusion.4 = f32[3,4096]{0,1:T(8,128)S(1)} fusion(f32[3,4096]{0,1:T(8,128)S(1)} %scatter_custom_fusion.3, s32[1024]{0:T(1024)S(1)} %bitcast.57, f32[]{:T(128)} %constant.7.clone.1, f32[1024,3]{1,0:T(8,128)S(1)} %bitcast.52, f32[1024,3]{1,0:T(8,128)S(1)} %bitcast.50), kind=kCustom, calls=%fused_computation.15 | custom fusion | flops 9216 | bytes 1097732 | tf_op jit(solution)/shard_map/scatter-add | solution.py:60
  129.6 1.3 copy-done
  131.0 0.0 reduce-scatter.5.cloned.1.call-update
  131.0 136.7 %reduce-scatter.5.cloned.1.call-done = f32[3,128]{0,1:T(8,128)} async-done(((f32[3,4096]{0,1:T(8,128)}), f32[3,128]{0,1:T(8,128)}) %reduce-scatter.5.cloned.1.call-update) | async-done | bytes 1552 | tf_op jit(solution)/shard_map/reduce_scatter | solution.py:61
  267.7 1.5 copy.20
  (17 shorter events, 0.1 us)
Async XLA Ops:
  6.5 0.7 copy-start.3
  6.5 47.8 %reduce-scatter.3.cloned.1.call-start = ((), (), s32[]{:S(2)}) async-start(), calls=%async_computation.4 | async-start | bytes 3522560 | tf_op jit(solution)/shard_map/reduce_scatter | solution.py:18
  15.7 47.2 %all-to-all-start = ((s32[8,1,256]{2,1,0:T(1,128)}), s32[8,1,256]{2,1,0:T(1,128)S(1)}, u32[]{:S(2)}, u32[]{:S(2)}) async-start(s32[8,1,256]{2,1,0:T(1,128)} %bitcast.4), calls=%async_computation | async-start | bytes 16384 | tf_op jit(solution)/shard_map/all_to_all | solution.py:39
  62.9 38.9 %all-to-all-start.1 = ((bf16[8,256,338]{1,2,0:T(8,128)(2,1)}), bf16[8,256,338]{1,2,0:T(8,128)(2,1)S(1)}, u32[]{:S(2)}, u32[]{:S(2)}) async-start(bf16[8,256,338]{1,2,0:T(8,128)(2,1)} %copy.17), calls=%async_computation.2 | async-start | bytes 2818048 | tf_op jit(solution)/shard_map/all_to_all | solution.py:32
  67.5 200.2 %reduce-scatter.5.cloned.1.call-start = ((), (), s32[]{:S(2)}) async-start(), calls=%async_computation.5 | async-start | bytes 2162688 | tf_op jit(solution)/shard_map/reduce_scatter | solution.py:61
  74.8 2.6 copy-start.4
  103.4 10.5 %copy-start.1 = (bf16[1024,3,169]{2,1,0:T(4,128)(2,1)S(1)}, bf16[1024,3,169]{2,1,0:T(4,128)(2,1)}, u32[]{:S(2)}) copy-start(bf16[1024,3,169]{2,1,0:T(4,128)(2,1)} %copy.25) | copy-start | bytes 3115012
  113.9 1.6 copy-start.2
  129.6 1.4 copy-start
Sparse Core Ops, SparseCore 0:
  10.4 43.8 reduce-scatter.2
  131.1 136.5 reduce-scatter.4
where the time goes:
time: 277 us; the launch traced here: 276 us
  waiting for transfers between devices  194 us (70%)
  local copies, waits for them, and re-layouts  39.5 us (14%)
  other arithmetic  15.5 us (6%)
  between operations  13.6 us (5%)
  starting transfers between devices  11 us (4%)
    reduce_scatter x1, waiting for transfers between devices, body(): lax.psum_scatter(partial_forces, ('pole', 'node'), scatter_dimension=1, t...  137 us
    reduce_scatter x1, waiting for transfers between devices, body(): lax.psum_scatter(partials, 'pole', scatter_dimension=0, tiled=True)  32.2 us
    all_to_all x1, waiting for transfers between devices, body(): lax.all_to_all(outgoing.reshape(nodes, capacity, width), 'node', split_ax...  24.4 us
    scatter x1, local copies, waits for them, and re-layouts, body(): pair_dens = jnp.zeros((blocks_here, width), jnp.bfloat16).at[recv_slot.re...  10.3 us
    scatter-add x1, other arithmetic, body(): partial_forces = partial_forces.at[:, pair_atoms[0]].add(-2.0 * pair_term.T)  6.59 us
    all_to_all x1, starting transfers between devices, body(): lax.all_to_all(sent_slot.reshape(nodes, capacity), 'node', split_axis=0,...  6.35 us
    scatter-add x1, other arithmetic, body(): partial_forces = partial_forces.at[:, pair_atoms[1]].add(2.0 * pair_term.T)  6.3 us
  transfers between devices with their start and end apart: 4, of which 3 were waited for; matrix products, arithmetic and copies ran while one was open for 10% of the time, Pallas kernels for 0%

commit v1 on v0

v1 whole, which is shorter than its diff:
```python
import functools

import jax
import jax.numpy as jnp
from jax import lax
from jax.experimental import pallas as pl
from jax.experimental.pallas import tpu as pltpu
from jax.sharding import PartitionSpec as P

LANES = 128
CHUNK = 128
ROWS = 8
DIGIT = 32
MESH = pl.DeviceIdType.MESH
NT = (((1,), (1,)), ((), ()))
F32 = jnp.float32
BF16 = jnp.bfloat16


def iota(shape, dim):
    return lax.broadcasted_iota(jnp.int32, shape, dim)


def onehot(cond):
    return jnp.where(cond, 1.0, 0.0).astype(BF16)


def split_two(x):
    high = x.astype(BF16)
    return high, (x - high.astype(F32)).astype(BF16)


def kernel(
    poles, nodes, blocks, width, cap,
    dens, node_ref, slot_ref, deriv, atoms, out,
    own, parts, dv, aligned, pack, place, ranks, slot_rows, slot_send, slot_recv,
    send_buf, recv_buf, density, acc, force, force_in, force_two, force_last,
    own_sem, dv_sem, rs_send, rs_recv, sl_send, sl_recv, ex_send, ex_recv,
    fa_send, fa_recv, fb_send, fb_recv,
):
    half = width // 2
    chunks = -(-width // CHUNK)
    total = deriv.shape[0]
    pole = lax.axis_index("pole")
    node = lax.axis_index("node")

    def near_first(i):
        return nodes // 2 + (1 - 2 * (i % 2)) * ((i + 1) // 2)

    def rows(t):
        return min(CHUNK, width - t * CHUNK)

    own_copies = []
    for t in range(chunks):
        copy = pltpu.make_async_copy(
            dens.at[pl.ds(t * CHUNK, rows(t)), pl.ds(pole * blocks, blocks)],
            own[t],
            own_sem.at[t],
        )
        own_copies.append(copy)
    dv_copy = pltpu.make_async_copy(deriv, dv, dv_sem)

    barrier = pltpu.get_barrier_semaphore()
    for r in range(1, poles):
        pl.semaphore_signal(
            barrier, inc=1, device_id={"pole": (pole + r) % poles}, device_id_type=MESH
        )

    @pl.loop(1, nodes)
    def _(k):
        pl.semaphore_signal(
            barrier, inc=1, device_id={"node": (node + k) % nodes}, device_id_type=MESH
        )

    for copy in own_copies:
        copy.start()
    dv_copy.start()
    pl.semaphore_wait(barrier, poles - 1 + nodes - 1)

    def rs_copy(t, r):
        dest = (pole + r) % poles
        return pltpu.make_async_remote_copy(
            src_ref=dens.at[pl.ds(t * CHUNK, rows(t)), pl.ds(dest * blocks, blocks)],
            dst_ref=parts[t].at[r - 1],
            send_sem=rs_send.at[t, r - 1],
            recv_sem=rs_recv.at[t, r - 1],
            device_id={"pole": dest},
            device_id_type=MESH,
        )

    for t in range(chunks):
        for r in range(1, poles):
            rs_copy(t, r).start()

    dest_row = node_ref[pl.ds(pole, 1), :]
    slot_row = slot_ref[pl.ds(pole, 1), :]
    hot = dest_row == iota((nodes, blocks), 0)
    before = onehot(iota((blocks, blocks), 0) < iota((blocks, blocks), 1))
    rank = jnp.dot(onehot(hot), before, preferred_element_type=F32)
    ranks[...] = jnp.where(hot, rank, -1.0)
    digit_high = (slot_row // DIGIT + 1).astype(F32)
    digit_low = (slot_row % DIGIT).astype(F32)
    which = iota((ROWS, blocks), 0)
    slot_rows[...] = jnp.where(
        which == 0, digit_high, jnp.where(which == 1, digit_low, 0.0)
    ).astype(BF16)

    def slot_copy(k):
        return pltpu.make_async_remote_copy(
            src_ref=slot_send.at[k],
            dst_ref=slot_recv.at[k],
            send_sem=sl_send.at[k],
            recv_sem=sl_recv.at[k],
            device_id={"node": (node + k) % nodes},
            device_id_type=MESH,
        )

    def make_pack(k):
        row = ranks[pl.ds((node + k) % nodes, 1), :]
        pack[k] = onehot(row == iota((cap, blocks), 0).astype(F32))
        return lax.dot_general(slot_rows[...], pack[k], NT, preferred_element_type=F32)

    @pl.loop(1, nodes)
    def _(k):
        slot_send[k] = make_pack(k)
        slot_copy(k).start()

    slot_recv[0] = make_pack(0)

    dv_copy.wait()
    wide = chunks * CHUNK
    for c in range(3):
        for start, first, sign in ((c * half, 0, 1.0), ((3 + c) * half, half, -1.0)):
            low = start // LANES * LANES
            high = min(-(-(start + half) // LANES) * LANES, total)
            src = iota((wide, high - low), 1) + (low - start)
            row = iota((wide, high - low), 0) - first
            moved = jnp.where((src == row) & (row >= 0) & (row < half), sign, 0.0).astype(BF16)
            piece = jnp.dot(moved, dv[low:high, :], preferred_element_type=F32)
            got = piece if first == 0 else got + piece
        aligned[c] = got.astype(BF16)

    def ex_copy(t, k):
        return pltpu.make_async_remote_copy(
            src_ref=send_buf[t].at[k],
            dst_ref=recv_buf[t].at[k],
            send_sem=ex_send.at[t, k],
            recv_sem=ex_recv.at[t, k],
            device_id={"node": (node + k) % nodes},
            device_id_type=MESH,
        )

    def exchange(t):
        own_copies[t].wait()
        for r in range(1, poles):
            rs_copy(t, r).wait_recv()
        summed = own[t][...].astype(F32)
        for r in range(1, poles):
            summed = summed + parts[t][r - 1].astype(F32)
        density[t][...] = summed.astype(BF16)

        def packed(k):
            return lax.dot_general(
                density[t][...], pack[k], NT, preferred_element_type=F32
            ).astype(BF16)

        @pl.loop(0, nodes - 1)
        def _(i):
            k = near_first(i)
            send_buf[t][k] = packed(k)
            ex_copy(t, k).start()

        recv_buf[t][0] = packed(0)

    def make_place(k):
        digits = slot_recv[k]
        slot = (digits[0:1, :] - 1.0) * DIGIT + digits[1:2, :]
        place[k] = onehot(slot == iota((blocks, cap), 0).astype(F32))

    def contract(t):
        def placed(k):
            return lax.dot_general(
                recv_buf[t][k], place[k], NT, preferred_element_type=F32
            )

        acc[t][...] = placed(0)

        @pl.loop(0, nodes - 1)
        def _(i):
            k = near_first(nodes - 2 - i)
            ex_copy(t, k).wait_recv()
            acc[t][...] += placed(k)

        sums = jnp.zeros((ROWS, blocks), F32)
        for c in range(3):
            prod = acc[t][...] * aligned[c, t * CHUNK:t * CHUNK + rows(t), :].astype(F32)
            sums = jnp.where(which == c, jnp.sum(prod, axis=0, keepdims=True), sums)
        return sums

    exchange(0)
    make_place(0)

    @pl.loop(1, nodes)
    def _(k):
        slot_copy(k).wait_recv()
        make_place(k)

    term = None
    for t in range(1, chunks):
        exchange(t)
        part = contract(t - 1)
        term = part if term is None else term + part
    part = contract(chunks - 1)
    term = part if term is None else term + part

    owners = poles * nodes
    group = min(owners, 32)
    height = group * ROWS
    pieces = split_two(2.0 * term)
    for g in range(owners // group):
        block = iota((height, blocks), 0) // ROWS + g * group
        owner = (block % poles) * nodes + block // poles
        result = None
        for end in range(2):
            atom = atoms[end:end + 1, :]
            low = onehot(atom % LANES == iota((LANES, blocks), 0))
            here = (atom // LANES) == owner
            for piece in pieces:
                value = jnp.tile(piece.astype(F32), (group, 1))
                lhs = jnp.where(here, value if end == 1 else -value, 0.0).astype(BF16)
                got = lax.dot_general(lhs, low, NT, preferred_element_type=F32)
                result = got if result is None else result + got
        span = group // poles
        force[g * span:(g + 1) * span] = result.reshape(span, poles, ROWS, LANES)

    def fa_copy(k):
        dest = (node + k) % nodes
        return pltpu.make_async_remote_copy(
            src_ref=force.at[dest],
            dst_ref=force_in.at[k],
            send_sem=fa_send.at[k],
            recv_sem=fa_recv.at[k],
            device_id={"node": dest},
            device_id_type=MESH,
        )

    @pl.loop(0, nodes - 1)
    def _(i):
        fa_copy(near_first(i)).start()

    force_two[...] = force[node]

    @pl.loop(0, nodes - 1)
    def _(i):
        k = near_first(nodes - 2 - i)
        fa_copy(k).wait_recv()
        force_two[...] += force_in[k]

    def fb_copy(r):
        dest = (pole + r) % poles
        return pltpu.make_async_remote_copy(
            src_ref=force_two.at[dest],
            dst_ref=force_last.at[r],
            send_sem=fb_send.at[r],
            recv_sem=fb_recv.at[r],
            device_id={"pole": dest},
            device_id_type=MESH,
        )

    for r in range(1, poles):
        fb_copy(r).start()
    final = force_two[pole]
    for r in range(1, poles):
        fb_copy(r).wait_recv()
        final = final + force_last[r]
    out[...] = final[0:3, :]

    for t in range(chunks):
        for r in range(1, poles):
            rs_copy(t, r).wait_send()

        @pl.loop(1, nodes)
        def _(k):
            ex_copy(t, k).wait_send()

    @pl.loop(1, nodes)
    def _(k):
        slot_copy(k).wait_send()
        fa_copy(k).wait_send()

    for r in range(1, poles):
        fb_copy(r).wait_send()


def body(dens_part, dest_node, pair_slot, deriv, pair_atoms):
    blocks = deriv.shape[0]
    total = deriv.shape[1]
    width = dens_part.shape[2]
    nodes = lax.axis_size("node")
    poles = lax.axis_size("pole")
    cap = 2 * blocks // nodes
    chunks = -(-width // CHUNK)
    sizes = [min(CHUNK, width - t * CHUNK) for t in range(chunks)]
    dma = pltpu.SemaphoreType.DMA
    vmem = pl.BlockSpec(memory_space=pltpu.VMEM)
    hbm = pl.BlockSpec(memory_space=pl.ANY)
    return pl.pallas_call(
        functools.partial(kernel, poles, nodes, blocks, width, cap),
        out_shape=jax.ShapeDtypeStruct((3, LANES), F32),
        in_specs=[hbm, vmem, vmem, hbm, vmem],
        out_specs=vmem,
        scratch_shapes=[
            [pltpu.VMEM((n, blocks), BF16) for n in sizes],
            [pltpu.VMEM((poles - 1, n, blocks), BF16) for n in sizes],
            pltpu.VMEM((total, blocks), BF16),
            pltpu.VMEM((3, chunks * CHUNK, blocks), BF16),
            pltpu.VMEM((nodes, cap, blocks), BF16),
            pltpu.VMEM((nodes, blocks, cap), BF16),
            pltpu.VMEM((nodes, blocks), F32),
            pltpu.VMEM((ROWS, blocks), BF16),
            pltpu.VMEM((nodes, ROWS, cap), F32),
            pltpu.VMEM((nodes, ROWS, cap), F32),
            [pltpu.VMEM((nodes, n, cap), BF16) for n in sizes],
            [pltpu.VMEM((nodes, n, cap), BF16) for n in sizes],
            [pltpu.VMEM((n, blocks), BF16) for n in sizes],
            [pltpu.VMEM((n, blocks), F32) for n in sizes],
            pltpu.VMEM((nodes, poles, ROWS, LANES), F32),
            pltpu.VMEM((nodes, poles, ROWS, LANES), F32),
            pltpu.VMEM((poles, ROWS, LANES), F32),
            pltpu.VMEM((poles, ROWS, LANES), F32),
            dma((chunks,)),
            dma,
            dma((chunks, poles - 1)),
            dma((chunks, poles - 1)),
            dma((nodes,)),
            dma((nodes,)),
            dma((chunks, nodes)),
            dma((chunks, nodes)),
            dma((nodes,)),
            dma((nodes,)),
            dma((poles,)),
            dma((poles,)),
        ],
        compiler_params=pltpu.CompilerParams(
            collective_id=0, has_side_effects=True, vmem_limit_bytes=60 << 20
        ),
    )(
        dens_part[0].T,
        dest_node.reshape(poles, blocks),
        pair_slot.reshape(poles, blocks),
        deriv.T,
        pair_atoms,
    )


def solution(mesh):
    return jax.shard_map(
        body,
        mesh=mesh,
        in_specs=(
            P("pole", "node", None),
            P("node"),
            P("node"),
            P(("pole", "node"), None),
            P(None, ("pole", "node")),
        ),
        out_specs=P(None, ("pole", "node")),
        check_vma=False,
    )
```

time: 277 us -> 66.3 us (0.24)
  waiting for transfers between devices: 194 us -> 0 us
  Pallas kernels: 0 us -> 61.9 us
  local copies, waits for them, and re-layouts: 39.5 us -> 3.88 us
  other arithmetic: 15.5 us -> 0 us
  between operations: 13.6 us -> 0.01 us
  starting transfers between devices: 11 us -> 0 us
    reduce_scatter x2 -> x0, waiting for transfers between devices: 169 us -> none  [the longest x1 137 us: body(): lax.psum_scatter(partial_forces, ('pole', 'node'), scatter_dimension=1, t...]
    pallas_call x0 -> x1, Pallas kernels: none -> 61.9 us  [body(): pl.pallas_call(functools.partial(kernel, poles, nodes, blocks, width, cap...]
    all_to_all x2 -> x0, waiting for transfers between devices: 24.4 us -> none  [the longest x1 24.4 us: body(): lax.all_to_all(outgoing.reshape(nodes, capacity, width), 'node', split_ax...]
    scatter x3 -> x0, local copies, waits for them, and re-layouts: 20.7 us -> none  [the longest x1 10.3 us: body(): pair_dens = jnp.zeros((blocks_here, width), jnp.bfloat16).at[recv_slot.re...]
    scatter-add x2 -> x0, other arithmetic: 12.9 us -> none  [the longest x1 6.59 us: body(): partial_forces = partial_forces.at[:, pair_atoms[0]].add(-2.0 * pair_term.T)]
    all_to_all x2 -> x0, starting transfers between devices: 10.9 us -> none  [the longest x1 6.35 us: body(): lax.all_to_all(sent_slot.reshape(nodes, capacity), 'node', split_axis=0,...]
    reshape x6 -> x2, local copies, waits for them, and re-layouts: 10 us -> 2.65 us  [the longest x1 1.33 us: body(): pair_slot.reshape(poles, blocks)]
    slice x3 -> x0, local copies, waits for them, and re-layouts: 3.47 us -> none  [the longest x1 2.93 us: body(): grad_s = deriv[:, 3 * half_width:].reshape(blocks_here, 3, half_width)]
  transfers between devices with their start and end apart: 4 -> 0, of which waited for: 3 -> 0; matrix products, arithmetic and copies ran while one was open for 10% -> 0% of each run, Pallas kernels for 0% -> 0%
where the time goes in v1:
time: 66.3 us; the launch traced here: 65.8 us
  Pallas kernels  61.9 us (93%)
  local copies, waits for them, and re-layouts  3.88 us (6%)
    pallas_call x1, Pallas kernels, body(): pl.pallas_call(functools.partial(kernel, poles, nodes, blocks, width, cap...  61.9 us

profile of v1, /device:TPU:0, one launch (start us, length us, event | category | flops | bytes accessed | tf_op | source)
XLA Modules:
  0.0 65.8 jit_solution(11511109945637929698)
XLA Ops:
  0.0 1.3 %reshape.6.node_ref = s32[4,1024]{1,0:T(4,128)} reshape(s32[4096]{0:T(1024)} %param.6) | data formatting | bytes 32768 | tf_op jit(solution)/shard_map/reshape | solution.py:349
  1.3 1.3 %reshape.7.slot_ref = s32[4,1024]{1,0:T(4,128)} reshape(s32[4096]{0:T(1024)} %param.7) | data formatting | bytes 32768 | tf_op jit(solution)/shard_map/reshape | solution.py:350
  2.6 61.9 %shard_map.55 = f32[3,128]{1,0:T(4,128)} custom-call(bf16[338,4096]{1,0:T(8,128)(2,1)} %bitcast.4, s32[4,1024]{1,0:T(4,128)} %reshape.6.node_ref, s32[4,1024]{1,0:T(4,128)} %reshape.7.slot_ref, bf16[1014,1024]{1,0:T(8,128)(2,1)} %bitcast.5, s32[2,1024]{1,0:T(2,128)} %atoms.1), custom_call_target="tpu_custom_call" | custom-call | tf_op jit(solution)/shard_map/pallas_call | solution.py:307
  64.6 1.2 %copy.7 = f32[3,128]{1,0:T(4,128)} copy(f32[3,128]{1,0:T(4,128)} %shard_map.55) | data formatting | bytes 3072

commit v2 on v1

--- a/solution.py
+++ b/solution.py
@@ -8,9 +8,10 @@
 from jax.sharding import PartitionSpec as P
 
 LANES = 128
-CHUNK = 128
+CHUNK = 96
 ROWS = 8
 DIGIT = 32
+PART = 4
 MESH = pl.DeviceIdType.MESH
 NT = (((1,), (1,)), ((), ()))
 F32 = jnp.float32
@@ -32,11 +33,11 @@
 
 def kernel(
     poles, nodes, blocks, width, cap,
-    dens, node_ref, slot_ref, deriv, atoms, out,
+    dens, node_hbm, slot_hbm, deriv, atoms, out,
     own, parts, dv, aligned, pack, place, ranks, slot_rows, slot_send, slot_recv,
     send_buf, recv_buf, density, acc, force, force_in, force_two, force_last,
     own_sem, dv_sem, rs_send, rs_recv, sl_send, sl_recv, ex_send, ex_recv,
-    fa_send, fa_recv, fb_send, fb_recv,
+    fa_send, fa_recv, fb_send, fb_recv, node_ref, slot_ref, int_sem,
 ):
     half = width // 2
     chunks = -(-width // CHUNK)
@@ -58,6 +59,10 @@
             own_sem.at[t],
         )
         own_copies.append(copy)
+    int_copies = [
+        pltpu.make_async_copy(ref.at[pl.ds(pole * blocks, blocks)], row.at[0], int_sem.at[i])
+        for i, (ref, row) in enumerate(((node_hbm, node_ref), (slot_hbm, slot_ref)))
+    ]
     dv_copy = pltpu.make_async_copy(deriv, dv, dv_sem)
 
     barrier = pltpu.get_barrier_semaphore()
@@ -72,7 +77,7 @@
             barrier, inc=1, device_id={"node": (node + k) % nodes}, device_id_type=MESH
         )
 
-    for copy in own_copies:
+    for copy in int_copies + own_copies:
         copy.start()
     dv_copy.start()
     pl.semaphore_wait(barrier, poles - 1 + nodes - 1)
@@ -92,8 +97,10 @@
         for r in range(1, poles):
             rs_copy(t, r).start()
 
-    dest_row = node_ref[pl.ds(pole, 1), :]
-    slot_row = slot_ref[pl.ds(pole, 1), :]
+    for copy in int_copies:
+        copy.wait()
+    dest_row = node_ref[...]
+    slot_row = slot_ref[...]
     hot = dest_row == iota((nodes, blocks), 0)
     before = onehot(iota((blocks, blocks), 0) < iota((blocks, blocks), 1))
     rank = jnp.dot(onehot(hot), before, preferred_element_type=F32)
@@ -194,7 +201,7 @@
         sums = jnp.zeros((ROWS, blocks), F32)
         for c in range(3):
             prod = acc[t][...] * aligned[c, t * CHUNK:t * CHUNK + rows(t), :].astype(F32)
-            sums = jnp.where(which == c, jnp.sum(prod, axis=0, keepdims=True), sums)
+            sums = jnp.where(which % PART == c, jnp.sum(prod, axis=0, keepdims=True), sums)
         return sums
 
     exchange(0)
@@ -215,10 +222,10 @@
 
     owners = poles * nodes
     group = min(owners, 32)
-    height = group * ROWS
+    height = group * PART
     pieces = split_two(2.0 * term)
     for g in range(owners // group):
-        block = iota((height, blocks), 0) // ROWS + g * group
+        block = iota((height, blocks), 0) // PART + g * group
         owner = (block % poles) * nodes + block // poles
         result = None
         for end in range(2):
@@ -226,12 +233,12 @@
             low = onehot(atom % LANES == iota((LANES, blocks), 0))
             here = (atom // LANES) == owner
             for piece in pieces:
-                value = jnp.tile(piece.astype(F32), (group, 1))
+                value = jnp.tile(piece.astype(F32), (group // 2, 1))
                 lhs = jnp.where(here, value if end == 1 else -value, 0.0).astype(BF16)
                 got = lax.dot_general(lhs, low, NT, preferred_element_type=F32)
                 result = got if result is None else result + got
         span = group // poles
-        force[g * span:(g + 1) * span] = result.reshape(span, poles, ROWS, LANES)
+        force[g * span:(g + 1) * span] = result.reshape(span, poles // 2, ROWS, LANES)
 
     def fa_copy(k):
         dest = (node + k) % nodes
@@ -259,7 +266,7 @@
     def fb_copy(r):
         dest = (pole + r) % poles
         return pltpu.make_async_remote_copy(
-            src_ref=force_two.at[dest],
+            src_ref=force_two.at[dest // 2],
             dst_ref=force_last.at[r],
             send_sem=fb_send.at[r],
             recv_sem=fb_recv.at[r],
@@ -269,11 +276,11 @@
 
     for r in range(1, poles):
         fb_copy(r).start()
-    final = force_two[pole]
+    final = force_two[pole // 2]
     for r in range(1, poles):
         fb_copy(r).wait_recv()
         final = final + force_last[r]
-    out[...] = final[0:3, :]
+    out[...] = jnp.where(pole % 2 == 0, final[0:3, :], final[PART:PART + 3, :])
 
     for t in range(chunks):
         for r in range(1, poles):
@@ -307,7 +314,7 @@
     return pl.pallas_call(
         functools.partial(kernel, poles, nodes, blocks, width, cap),
         out_shape=jax.ShapeDtypeStruct((3, LANES), F32),
-        in_specs=[hbm, vmem, vmem, hbm, vmem],
+        in_specs=[hbm, hbm, hbm, hbm, vmem],
         out_specs=vmem,
         scratch_shapes=[
             [pltpu.VMEM((n, blocks), BF16) for n in sizes],
@@ -324,9 +331,9 @@
             [pltpu.VMEM((nodes, n, cap), BF16) for n in sizes],
             [pltpu.VMEM((n, blocks), BF16) for n in sizes],
             [pltpu.VMEM((n, blocks), F32) for n in sizes],
-            pltpu.VMEM((nodes, poles, ROWS, LANES), F32),
-            pltpu.VMEM((nodes, poles, ROWS, LANES), F32),
-            pltpu.VMEM((poles, ROWS, LANES), F32),
+            pltpu.VMEM((nodes, poles // 2, ROWS, LANES), F32),
+            pltpu.VMEM((nodes, poles // 2, ROWS, LANES), F32),
+            pltpu.VMEM((poles // 2, ROWS, LANES), F32),
             pltpu.VMEM((poles, ROWS, LANES), F32),
             dma((chunks,)),
             dma,
@@ -340,14 +347,17 @@
             dma((nodes,)),
             dma((poles,)),
             dma((poles,)),
+            pltpu.VMEM((1, blocks), jnp.int32),
+            pltpu.VMEM((1, blocks), jnp.int32),
+            dma((2,)),
         ],
         compiler_params=pltpu.CompilerParams(
             collective_id=0, has_side_effects=True, vmem_limit_bytes=60 << 20
         ),
     )(
         dens_part[0].T,
-        dest_node.reshape(poles, blocks),
-        pair_slot.reshape(poles, blocks),
+        dest_node,
+        pair_slot,
         deriv.T,
         pair_atoms,
     )

time: 66.3 us -> 61 us (0.920)
  local copies, waits for them, and re-layouts: 3.88 us -> 1.26 us
  Pallas kernels: 61.9 us -> 59.5 us
    reshape x2 -> x0, local copies, waits for them, and re-layouts: 2.65 us -> none  [the longest x1 1.33 us: body(): pair_slot.reshape(poles, blocks)]
    pallas_call x1, Pallas kernels: 61.9 us -> 59.5 us  [body(): pl.pallas_call(functools.partial(kernel, poles, nodes, blocks, width, cap...]
where the time goes in v2:
time: 61 us; the launch traced here: 60.8 us
  Pallas kernels  59.5 us (98%)
  local copies, waits for them, and re-layouts  1.26 us (2%)
    pallas_call x1, Pallas kernels, body(): pl.pallas_call(functools.partial(kernel, poles, nodes, blocks, width, cap...  59.5 us
    unnamed x1, local copies, waits for them, and re-layouts  1.26 us

profile of v2, /device:TPU:0, one launch (start us, length us, event | category | flops | bytes accessed | tf_op | source)
XLA Modules:
  0.0 60.8 jit_solution(14972670388412929395)
XLA Ops:
  0.0 59.5 %shard_map.55 = f32[3,128]{1,0:T(4,128)} custom-call(bf16[338,4096]{1,0:T(8,128)(2,1)} %bitcast.4, s32[4096]{0:T(1024)} %node_hbm.1, s32[4096]{0:T(1024)} %slot_hbm.1, bf16[1014,1024]{1,0:T(8,128)(2,1)} %bitcast.5, s32[2,1024]{1,0:T(2,128)} %atoms.1), custom_call_target="tpu_custom_call" | custom-call | tf_op jit(solution)/shard_map/pallas_call | solution.py:314
  59.5 1.3 %copy.7 = f32[3,128]{1,0:T(4,128)} copy(f32[3,128]{1,0:T(4,128)} %shard_map.55) | data formatting | bytes 3072

commit v3 on v2

--- a/solution.py
+++ b/solution.py
@@ -34,9 +34,9 @@
 def kernel(
     poles, nodes, blocks, width, cap,
     dens, node_hbm, slot_hbm, deriv, atoms, out,
-    own, parts, dv, aligned, pack, place, ranks, slot_rows, slot_send, slot_recv,
+    own, first_in, mid, second_in, dv, aligned, pack, place, ranks, slot_rows, slot_send, slot_recv,
     send_buf, recv_buf, density, acc, force, force_in, force_two, force_last,
-    own_sem, dv_sem, rs_send, rs_recv, sl_send, sl_recv, ex_send, ex_recv,
+    own_sem, dv_sem, one_send, one_recv, two_send, two_recv, sl_send, sl_recv, ex_send, ex_recv,
     fa_send, fa_recv, fb_send, fb_recv, node_ref, slot_ref, int_sem,
 ):
     half = width // 2
@@ -51,14 +51,66 @@
     def rows(t):
         return min(CHUNK, width - t * CHUNK)
 
-    own_copies = []
-    for t in range(chunks):
-        copy = pltpu.make_async_copy(
-            dens.at[pl.ds(t * CHUNK, rows(t)), pl.ds(pole * blocks, blocks)],
-            own[t],
-            own_sem.at[t],
-        )
-        own_copies.append(copy)
+    digits = (pole % 2, pole // 2)
+
+    def index(stripe, first, second):
+        return second * 2 + first if stripe == 0 else first * 2 + second
+
+    def stripe_rows(t, stripe):
+        top = rows(t) // 2 // 16 * 16
+        return (0, top) if stripe == 0 else (top, rows(t) - top)
+
+    def source(t, stripe, share):
+        start, size = stripe_rows(t, stripe)
+        return dens.at[pl.ds(t * CHUNK + start, size), pl.ds(share * blocks, blocks)]
+
+    def own_copy(t, stripe, e):
+        return pltpu.make_async_copy(
+            source(t, stripe, index(stripe, digits[stripe], e)),
+            own[t][stripe].at[e],
+            own_sem.at[t, stripe, e],
+        )
+
+    def one_copy(t, stripe, e):
+        there = 1 - digits[stripe]
+        return pltpu.make_async_remote_copy(
+            src_ref=source(t, stripe, index(stripe, there, e)),
+            dst_ref=first_in[t][stripe].at[e],
+            send_sem=one_send.at[t, stripe, e],
+            recv_sem=one_recv.at[t, stripe, e],
+            device_id={"pole": index(stripe, there, digits[1 - stripe])},
+            device_id_type=MESH,
+        )
+
+    def two_copy(t, stripe):
+        return pltpu.make_async_remote_copy(
+            src_ref=mid[t][stripe],
+            dst_ref=second_in[t][stripe],
+            send_sem=two_send.at[t, stripe],
+            recv_sem=two_recv.at[t, stripe],
+            device_id={"pole": index(stripe, digits[stripe], 1 - digits[1 - stripe])},
+            device_id_type=MESH,
+        )
+
+    def start_one(t):
+        if t < chunks:
+            for e in (1, 0):
+                for stripe in range(2):
+                    mine = digits[1 - stripe]
+                    one_copy(t, stripe, 1 - mine if e == 1 else mine).start()
+
+    def sum_two(t, stripe, e):
+        own_copy(t, stripe, e).wait()
+        one_copy(t, stripe, e).wait_recv()
+        return own[t][stripe][e].astype(F32) + first_in[t][stripe][e].astype(F32)
+
+    def middle(t):
+        if t < chunks:
+            for stripe in range(2):
+                mid[t][stripe][...] = sum_two(t, stripe, 1 - digits[1 - stripe]).astype(BF16)
+                two_copy(t, stripe).start()
+            start_one(t + 2)
+
     int_copies = [
         pltpu.make_async_copy(ref.at[pl.ds(pole * blocks, blocks)], row.at[0], int_sem.at[i])
         for i, (ref, row) in enumerate(((node_hbm, node_ref), (slot_hbm, slot_ref)))
@@ -77,25 +129,17 @@
             barrier, inc=1, device_id={"node": (node + k) % nodes}, device_id_type=MESH
         )
 
-    for copy in int_copies + own_copies:
+    for copy in int_copies:
         copy.start()
+    for t in range(chunks):
+        for stripe in range(2):
+            for e in range(2):
+                own_copy(t, stripe, e).start()
     dv_copy.start()
     pl.semaphore_wait(barrier, poles - 1 + nodes - 1)
 
-    def rs_copy(t, r):
-        dest = (pole + r) % poles
-        return pltpu.make_async_remote_copy(
-            src_ref=dens.at[pl.ds(t * CHUNK, rows(t)), pl.ds(dest * blocks, blocks)],
-            dst_ref=parts[t].at[r - 1],
-            send_sem=rs_send.at[t, r - 1],
-            recv_sem=rs_recv.at[t, r - 1],
-            device_id={"pole": dest},
-            device_id_type=MESH,
-        )
-
-    for t in range(chunks):
-        for r in range(1, poles):
-            rs_copy(t, r).start()
+    start_one(0)
+    start_one(1)
 
     for copy in int_copies:
         copy.wait()
@@ -158,13 +202,12 @@
         )
 
     def exchange(t):
-        own_copies[t].wait()
-        for r in range(1, poles):
-            rs_copy(t, r).wait_recv()
-        summed = own[t][...].astype(F32)
-        for r in range(1, poles):
-            summed = summed + parts[t][r - 1].astype(F32)
-        density[t][...] = summed.astype(BF16)
+        for stripe in range(2):
+            start, size = stripe_rows(t, stripe)
+            summed = sum_two(t, stripe, digits[1 - stripe])
+            two_copy(t, stripe).wait_recv()
+            summed = summed + second_in[t][stripe][...].astype(F32)
+            density[t][start:start + size, :] = summed.astype(BF16)
 
         def packed(k):
             return lax.dot_general(
@@ -180,8 +223,8 @@
         recv_buf[t][0] = packed(0)
 
     def make_place(k):
-        digits = slot_recv[k]
-        slot = (digits[0:1, :] - 1.0) * DIGIT + digits[1:2, :]
+        pair = slot_recv[k]
+        slot = (pair[0:1, :] - 1.0) * DIGIT + pair[1:2, :]
         place[k] = onehot(slot == iota((blocks, cap), 0).astype(F32))
 
     def contract(t):
@@ -204,6 +247,8 @@
             sums = jnp.where(which % PART == c, jnp.sum(prod, axis=0, keepdims=True), sums)
         return sums
 
+    middle(0)
+    middle(1)
     exchange(0)
     make_place(0)
 
@@ -212,13 +257,14 @@
         slot_copy(k).wait_recv()
         make_place(k)
 
-    term = None
+    term = jnp.zeros((ROWS, blocks), F32)
     for t in range(1, chunks):
+        middle(t + 1)
         exchange(t)
-        part = contract(t - 1)
-        term = part if term is None else term + part
-    part = contract(chunks - 1)
-    term = part if term is None else term + part
+        if t >= 3:
+            term = term + contract(t - 3)
+    for t in range(max(0, chunks - 3), chunks):
+        term = term + contract(t)
 
     owners = poles * nodes
     group = min(owners, 32)
@@ -283,8 +329,10 @@
     out[...] = jnp.where(pole % 2 == 0, final[0:3, :], final[PART:PART + 3, :])
 
     for t in range(chunks):
-        for r in range(1, poles):
-            rs_copy(t, r).wait_send()
+        for stripe in range(2):
+            two_copy(t, stripe).wait_send()
+            for e in range(2):
+                one_copy(t, stripe, e).wait_send()
 
         @pl.loop(1, nodes)
         def _(k):
@@ -308,6 +356,7 @@
     cap = 2 * blocks // nodes
     chunks = -(-width // CHUNK)
     sizes = [min(CHUNK, width - t * CHUNK) for t in range(chunks)]
+    stripes = [(n // 2 // 16 * 16, n - n // 2 // 16 * 16) for n in sizes]
     dma = pltpu.SemaphoreType.DMA
     vmem = pl.BlockSpec(memory_space=pltpu.VMEM)
     hbm = pl.BlockSpec(memory_space=pl.ANY)
@@ -317,8 +366,10 @@
         in_specs=[hbm, hbm, hbm, hbm, vmem],
         out_specs=vmem,
         scratch_shapes=[
-            [pltpu.VMEM((n, blocks), BF16) for n in sizes],
-            [pltpu.VMEM((poles - 1, n, blocks), BF16) for n in sizes],
+            [[pltpu.VMEM((2, n, blocks), BF16) for n in pair] for pair in stripes],
+            [[pltpu.VMEM((2, n, blocks), BF16) for n in pair] for pair in stripes],
+            [[pltpu.VMEM((n, blocks), BF16) for n in pair] for pair in stripes],
+            [[pltpu.VMEM((n, blocks), BF16) for n in pair] for pair in stripes],
             pltpu.VMEM((total, blocks), BF16),
             pltpu.VMEM((3, chunks * CHUNK, blocks), BF16),
             pltpu.VMEM((nodes, cap, blocks), BF16),
@@ -335,10 +386,12 @@
             pltpu.VMEM((nodes, poles // 2, ROWS, LANES), F32),
             pltpu.VMEM((poles // 2, ROWS, LANES), F32),
             pltpu.VMEM((poles, ROWS, LANES), F32),
-            dma((chunks,)),
+            dma((chunks, 2, 2)),
             dma,
-            dma((chunks, poles - 1)),
-            dma((chunks, poles - 1)),
+            dma((chunks, 2, 2)),
+            dma((chunks, 2, 2)),
+            dma((chunks, 2)),
+            dma((chunks, 2)),
             dma((nodes,)),
             dma((nodes,)),
             dma((chunks, nodes)),

time: 61 us -> 63.3 us (1.038)
  Pallas kernels: 59.5 us -> 61.9 us
    pallas_call x1, Pallas kernels: 59.5 us -> 61.9 us  [body(): pl.pallas_call(functools.partial(kernel, poles, nodes, blocks, width, cap...]
where the time goes in v3:
time: 63.3 us; the launch traced here: 63.1 us
  Pallas kernels  61.9 us (98%)
  local copies, waits for them, and re-layouts  1.26 us (2%)
    pallas_call x1, Pallas kernels, body(): pl.pallas_call(functools.partial(kernel, poles, nodes, blocks, width, cap...  61.9 us

profile of v3, /device:TPU:0, one launch (start us, length us, event | category | flops | bytes accessed | tf_op | source)
XLA Modules:
  0.0 63.1 jit_solution(10160115293184694147)
XLA Ops:
  0.0 61.9 %shard_map.55 = f32[3,128]{1,0:T(4,128)} custom-call(bf16[338,4096]{1,0:T(8,128)(2,1)} %bitcast.4, s32[4096]{0:T(1024)} %node_hbm.1, s32[4096]{0:T(1024)} %slot_hbm.1, bf16[1014,1024]{1,0:T(8,128)(2,1)} %bitcast.5, s32[2,1024]{1,0:T(2,128)} %atoms.1), custom_call_target="tpu_custom_call" | custom-call | tf_op jit(solution)/shard_map/pallas_call | solution.py:363
  61.9 1.3 %copy.7 = f32[3,128]{1,0:T(4,128)} copy(f32[3,128]{1,0:T(4,128)} %shard_map.55) | data formatting | bytes 3072

commit v4 on v2

--- a/solution.py
+++ b/solution.py
@@ -212,13 +212,13 @@
         slot_copy(k).wait_recv()
         make_place(k)
 
-    term = None
+    term = jnp.zeros((ROWS, blocks), F32)
     for t in range(1, chunks):
         exchange(t)
-        part = contract(t - 1)
-        term = part if term is None else term + part
-    part = contract(chunks - 1)
-    term = part if term is None else term + part
+        if t >= 3:
+            term = term + contract(t - 3)
+    for t in range(max(0, chunks - 3), chunks):
+        term = term + contract(t)
 
     owners = poles * nodes
     group = min(owners, 32)

time: 61 us -> 61.7 us (1.011)
  Pallas kernels: 59.5 us -> 60.3 us
    pallas_call x1, Pallas kernels: 59.5 us -> 60.3 us  [body(): pl.pallas_call(functools.partial(kernel, poles, nodes, blocks, width, cap...]
where the time goes in v4:
time: 61.7 us; the launch traced here: 61.5 us
  Pallas kernels  60.3 us (98%)
  local copies, waits for them, and re-layouts  1.26 us (2%)
    pallas_call x1, Pallas kernels, body(): pl.pallas_call(functools.partial(kernel, poles, nodes, blocks, width, cap...  60.3 us
    unnamed x1, local copies, waits for them, and re-layouts  1.26 us

profile of v4, /device:TPU:0, one launch (start us, length us, event | category | flops | bytes accessed | tf_op | source)
XLA Modules:
  0.0 61.5 jit_solution(497417651482492397)
XLA Ops:
  0.0 60.3 %shard_map.55 = f32[3,128]{1,0:T(4,128)} custom-call(bf16[338,4096]{1,0:T(8,128)(2,1)} %bitcast.4, s32[4096]{0:T(1024)} %node_hbm.1, s32[4096]{0:T(1024)} %slot_hbm.1, bf16[1014,1024]{1,0:T(8,128)(2,1)} %bitcast.5, s32[2,1024]{1,0:T(2,128)} %atoms.1), custom_call_target="tpu_custom_call" | custom-call | tf_op jit(solution)/shard_map/pallas_call | solution.py:314
  60.3 1.3 %copy.7 = f32[3,128]{1,0:T(4,128)} copy(f32[3,128]{1,0:T(4,128)} %shard_map.55) | data formatting | bytes 3072
